TPU v7x, 256 devices: a whole 4x4x8 slice. The times are simulated.
256 devices in a mesh: rows: 4 (over y), half: 2 (over core), obs: 32 (over z, x).
Axes of the slice: x: 4, y: 4, z: 8, core: 2. Of those that a mesh axis runs over, the one named last changes fastest.
Arguments:
- ens_state: bfloat16 [2, 8192, 256], P('half', ('rows', 'obs')), may hold values from -6 to 6
- state_pos: bfloat16 [8192], P(('rows', 'obs')), may hold values from 0 to 1
- obs_ens: bfloat16 [2, 2, 65536, 256], P(None, 'half', ('rows', 'obs')), may hold values from -6 to 6
- obs_pos: bfloat16 [2, 65536], P(None, ('rows', 'obs')), may hold values from 0 to 1
- innov_weight: bfloat16 [2, 2, 65536, 256], P(None, 'half', ('rows', 'obs')), may hold values from -0.875 to 0.875
- block_rows: int32 [2, 512, 16], replicated, may hold values from 0 to 63, as said below
Outputs:
- increment: float32 [2, 8192, 256], P('half', ('rows', 'obs'))
Inputs may be any that keep to these rules, and one draw needn't show every extreme that they name: `block_rows`: each row lists 16 different state blocks. Counting state blocks in aligned ranges of 16, an observation block names at most 8 blocks of one range, and in every aligned group of 16 observation blocks some range is named exactly 8 times by each block of the group.
All inputs are finite; a program needn't handle non-finite values.
Results may differ from a plain program's by a relative error of at most 0.0029.
Values may be sent and summed in bfloat16 or wider, within the bound.
No kernel may reach another device: no remote copies, remote signals or barrier semaphores. Data moves between devices by JAX's collectives and lax.ppermute only.
A program may use at most 64 MiB of HBM per device.

v0:
```python
import jax
import jax.numpy as jnp
from jax import lax
from jax.sharding import PartitionSpec as P

ROW_BLOCKS = 16
OBS_BLOCKS = 16
BATCHES = 2


def partner(value, axis, bit):
    mask = 2**bit
    pairs = [(source, source ^ mask) for source in range(lax.axis_size(axis))]
    return lax.ppermute(value, axis, pairs)


def slot_tables(picked, first_block, row_blocks):
    blocks_iota = jnp.arange(row_blocks, dtype=jnp.int32)
    relative = picked - first_block
    present = jnp.sum(
        (relative[:, :, None] == blocks_iota[None, None, :]).astype(jnp.int32), axis=1
    )
    ranking = jnp.cumsum(present, axis=1) - 1
    slot_iota = jnp.arange(row_blocks // 2, dtype=jnp.int32)
    chosen = present[:, :, None] * (ranking[:, :, None] == slot_iota[None, None, :]).astype(
        jnp.int32
    )
    slot_block = jnp.sum(chosen * blocks_iota[None, :, None], axis=1)
    slot_live = jnp.sum(chosen, axis=1)
    return (slot_block, slot_live)


def batch_increment(state_rows, row_places, obs_rows, obs_places, weights, picked, first_block):
    row_blocks = ROW_BLOCKS
    edge_size = obs_rows.shape[0] // picked.shape[0]
    member_count = state_rows.shape[1]
    state_tiles = state_rows.reshape(row_blocks, edge_size, member_count)
    place_tiles = row_places.astype(jnp.float32).reshape(row_blocks, edge_size)
    slot_block, slot_live = slot_tables(picked, first_block, row_blocks)

    def visit(running, entries):
        obs_tile, obs_place, weight_tile, blocks_here, live_here = entries
        gathered = state_tiles[blocks_here].reshape(-1, member_count)
        positions = place_tiles[blocks_here].reshape(-1)
        products = lax.dot_general(
            gathered, obs_tile, (((1,), (1,)), ((), ())), preferred_element_type=jnp.float32
        )
        distance = positions[:, None] - obs_place[None, :]
        damping = jnp.exp(-4.0 * distance * distance)
        live_rows = jnp.repeat(live_here.astype(jnp.float32), edge_size)
        scaled = (products * damping / (member_count - 1) * live_rows[:, None]).astype(jnp.bfloat16)
        additions = jnp.dot(scaled, weight_tile, preferred_element_type=jnp.float32)
        running = running.at[blocks_here].add(additions.reshape(-1, edge_size, member_count))
        return (running, None)

    initial = jnp.zeros((row_blocks, edge_size, member_count), jnp.float32)
    entries = (
        obs_rows.reshape(-1, edge_size, member_count),
        obs_places.astype(jnp.float32).reshape(-1, edge_size),
        weights.reshape(-1, edge_size, member_count),
        slot_block,
        slot_live,
    )
    running, _ = lax.scan(visit, initial, entries)
    return running.reshape(row_blocks * edge_size, member_count)


def local(ens_state, state_pos, obs_ens, obs_pos, innov_weight, block_rows):
    state_own, obs_own = (ens_state, obs_ens)
    weight_own = partner(innov_weight, "half", 0)
    place_column = obs_pos[:, None, :, None]
    obs_full, weight_full, place_full_obs = (
        lax.all_gather(obs_own, "rows", axis=2, tiled=True),
        lax.all_gather(weight_own, "rows", axis=2, tiled=True),
        lax.all_gather(place_column, "rows", axis=2, tiled=True),
    )
    state_full, place_full = (
        lax.all_gather(state_own[0], "obs", axis=0, tiled=True),
        lax.all_gather(state_pos, "obs", axis=0, tiled=True),
    )
    first_block = lax.axis_index("rows") * ROW_BLOCKS
    obs_count = lax.axis_size("obs")
    row_count = lax.axis_size("rows")
    span_blocks = OBS_BLOCKS // row_count
    block_ids = (
        (jnp.arange(row_count, dtype=jnp.int32)[:, None] * obs_count + lax.axis_index("obs"))
        * span_blocks
        + jnp.arange(span_blocks, dtype=jnp.int32)[None, :]
    ).reshape(-1)
    shares = None
    summed = None
    for batch_index in range(BATCHES):
        picked_here = block_rows[batch_index][block_ids]
        partial_value = batch_increment(
            state_full,
            place_full,
            obs_full[batch_index, 0],
            place_full_obs[batch_index, 0, :, 0],
            weight_full[batch_index, 0],
            picked_here,
            first_block,
        )
        summed = partial_value if summed is None else summed + partial_value
    shares = lax.psum_scatter(summed, "obs", scatter_dimension=0, tiled=True)
    shares = partner(shares, "half", 0)
    return shares[None]


def solution(mesh):
    in_specs = (
        P("half", ("rows", "obs"), None),
        P(("rows", "obs")),
        P(None, "half", ("rows", "obs"), None),
        P(None, ("rows", "obs")),
        P(None, "half", ("rows", "obs"), None),
        P(),
    )
    out_specs = P("half", ("rows", "obs"), None)
    return jax.shard_map(local, mesh=mesh, in_specs=in_specs, out_specs=out_specs, check_vma=False)
```

profile of v0, /device:TPU:1, one launch (start us, length us, event | category | flops | bytes accessed | tf_op | source)
XLA Modules:
  0.0 588.6 jit_solution(8644609748980073932)
XLA Ops:
  7.3 3.3 collective-permute-start
  18.8 62.3 %all-reduce = bf16[2048]{0:T(1024)(128)(2,1)S(1)} all-reduce(bf16[2048]{0:T(1024)(128)(2,1)S(1)} %dynamic-update-slice), channel_id=1, replica_groups=mesh['rows'=4,'half'=2,'obs'=32] {'obs'}, use_global_device_ids=true, to_apply=%add | all-reduce | flops 2048 | bytes 8192
  81.0 8.7 %all-gather.1 = bf16[2,2048]{1,0:T(2,128)(2,1)S(1)} all-gather(bf16[2,512]{1,0:T(2,128)(2,1)S(1)} %copy-done.2), channel_id=3, replica_groups=mesh['rows'=4,'half'=2,'obs'=32] {'rows'}, dimensions={1}, use_global_device_ids=true | all-gather | bytes 10240 | tf_op jit(solution)/shard_map/all_gather | solution.py:75
  90.7 3.0 fusion.36
  93.7 3.0 fusion.35
  96.7 58.7 %all-gather.10.cloned.1.call-done = bf16[1,2048,256]{2,1,0:T(8,128)(2,1)} async-done(((bf16[1,64,256]{2,1,0:T(8,128)(2,1)}), bf16[1,2048,256]{2,1,0:T(8,128)(2,1)}) %all-gather.10.cloned.1.call-update) | async-done | bytes 1048592 | tf_op jit(solution)/shard_map/all_gather | solution.py:78
  155.6 99.0 %while.21 = (s32[]{:T(128)}, f32[16,128,256]{2,1,0:T(8,128)S(1)}, s32[16,8]{1,0:T(8,128)S(1)}, bf16[16,128,256]{2,1,0:T(8,128)(2,1)}, bf16[16,128,256]{2,1,0:T(8...) while((s32[]{:T(128)}, f32[16,128,256]{2,1,0:T(8,128)S(1)}, ...), condition=%wide.region_13.14_spmd, body=%wide.region_11.13_spmd.sunk | while | flops 135267360 | bytes 6450065 | solution.py:64
  155.7 1.8 gather_fusion.2
  161.9 1.8 gather_fusion.2
  168.1 1.8 gather_fusion.2
  174.3 1.8 gather_fusion.2
  180.5 1.8 gather_fusion.2
  186.7 1.8 gather_fusion.2
  199.0 1.8 gather_fusion.2
  211.4 1.8 gather_fusion.2
  217.6 1.8 gather_fusion.2
  223.8 1.8 gather_fusion.2
  230.0 1.8 gather_fusion.2
  242.4 1.8 gather_fusion.2
  248.5 1.8 gather_fusion.2
  256.2 99.1 %while.20 = (s32[]{:T(128)}, f32[16,128,256]{2,1,0:T(8,128)S(1)}, s32[16,8]{1,0:T(8,128)S(1)}, bf16[16,128,256]{2,1,0:T(8,128)(2,1)}, bf16[16,128,256]{2,1,0:T(8...) while((s32[]{:T(128)}, f32[16,128,256]{2,1,0:T(8,128)S(1)}, ...), condition=%wide.region_6.7_spmd, body=%wide.region_4.6_spmd.sunk | while | flops 135267360 | bytes 6450065 | solution.py:64
  355.3 3.3 add.105
  358.6 215.7 %reduce-scatter.2.cloned.1.call-done = f32[64,256]{1,0:T(8,128)} async-done(((f32[2048,256]{1,0:T(8,128)}), f32[64,256]{1,0:T(8,128)}) %reduce-scatter.2.cloned.1.call-update) | async-done | bytes 65552 | tf_op jit(solution)/shard_map/reduce_scatter | solution.py:104
  574.4 6.0 %collective-permute-start.1 = (f32[64,256]{1,0:T(8,128)}, f32[64,256]{1,0:T(8,128)S(1)}, u32[]{:S(2)}, u32[]{:S(2)}) collective-permute-start(f32[64,256]{1,0:T(8,128)} %reduce-scatter.2.cloned.1.call-done), channel_id=1, source_target_pairs={{0,32},{32,0},{1,33},{33,1},{2,34},{34,2},{3,35},{35,3},{4,36},{36... | collective-permute-start | bytes 196616 | tf_op jit(solution)/shard_map/ppermute | solution.py:14
  (356 shorter events, 185.2 us)
Async XLA Ops:
  6.5 10.7 %copy-start.4 = (u32[256]{0:T(256)S(1)}, u32[256]{0:T(256)}, u32[]{:S(2)}) copy-start(u32[256]{0:T(256)} %constant.78) | copy-start | bytes 3076
  6.5 12.0 %copy-start.3 = (bf16[64]{0:T(256)(128)(2,1)S(1)}, bf16[64]{0:T(256)(128)(2,1)}, u32[]{:S(2)}) copy-start(bf16[64]{0:T(256)(128)(2,1)} %param.11) | copy-start | bytes 388
  6.5 74.5 %copy-start.2 = (bf16[2,512]{1,0:T(2,128)(2,1)S(1)}, bf16[2,512]{1,0:T(2,128)(2,1)}, u32[]{:S(2)}) copy-start(bf16[2,512]{1,0:T(2,128)(2,1)} %param.13) | copy-start | bytes 6148
  6.5 84.2 %all-gather.6.cloned.1.call-start = ((), (), s32[]{:S(2)}) async-start(), calls=%async_computation.1 | async-start | bytes 2621440 | tf_op jit(solution)/shard_map/all_gather | solution.py:73
  7.3 86.5 %all-gather.8.cloned.1.call-start = ((), (), s32[]{:S(2)}) async-start(), calls=%async_computation.2 | async-start | bytes 2621440 | tf_op jit(solution)/shard_map/all_gather | solution.py:74
  7.3 5.0 collective-permute-start
  12.3 0.8 copy-start.1
  13.2 142.3 %all-gather.10.cloned.1.call-start = ((), (), s32[]{:S(2)}) async-start(), calls=%async_computation.4 | async-start | bytes 1081344 | tf_op jit(solution)/shard_map/all_gather | solution.py:78
  13.9 560.5 %reduce-scatter.2.cloned.1.call-start = ((), (), s32[]{:S(2)}) async-start(), calls=%async_computation.3 | async-start | bytes 2162688 | tf_op jit(solution)/shard_map/reduce_scatter | solution.py:104
  254.7 1.4 copy-start
  574.4 7.1 %collective-permute-start.1 = (f32[64,256]{1,0:T(8,128)}, f32[64,256]{1,0:T(8,128)S(1)}, u32[]{:S(2)}, u32[]{:S(2)}) collective-permute-start(f32[64,256]{1,0:T(8,128)} %reduce-scatter.2.cloned.1.call-done), channel_id=1, source_target_pairs={{0,32},{32,0},{1,33},{33,1},{2,34},{34,2},{3,35},{35,3},{4,36},{36... | collective-permute-start | bytes 196616 | tf_op jit(solution)/shard_map/ppermute | solution.py:14
Sparse Core Ops, SparseCore 0:
  9.1 36.9 all-gather.5
  48.0 33.3 all-gather.7
  84.0 71.4 all-gather.9
  358.8 215.5 reduce-scatter.1
where the time goes:
time: 593 us; the launch traced here: 589 us
  waiting for transfers between devices  279 us (47%)
  local copies, waits for them, and re-layouts  90.2 us (15%)
  matrix products  74.5 us (13%)
  blocking collectives  71 us (12%)
  other arithmetic  48.8 us (8%)
  between operations  13.9 us (2%)
  starting transfers between devices  9.42 us (2%)
    reduce_scatter x1, waiting for transfers between devices, local(): shares = lax.psum_scatter(summed, 'obs', scatter_dimension=0, tiled=True)  216 us
    unnamed x1, blocking collectives  62.3 us
    all_gather x1, waiting for transfers between devices, local(): lax.all_gather(state_own[0], 'obs', axis=0, tiled=True)  58.7 us
    gather x32, local copies, waits for them, and re-layouts, visit(): gathered = state_tiles[blocks_here].reshape(-1, member_count)  57.8 us
    scatter-add x32, other arithmetic, visit(): running.at[blocks_here].add(additions.reshape(-1, edge_size, member_count))  42.6 us
    dot_general x32, matrix products, visit(): lax.dot_general(gathered, obs_tile, (((1,), (1,)), ((), ())), preferred_e...  38.7 us
    dot_general x32, matrix products, visit(): additions = jnp.dot(scaled, weight_tile, preferred_element_type=jnp.float32)  35.8 us
    gather x32, local copies, waits for them, and re-layouts, visit(): positions = place_tiles[blocks_here].reshape(-1)  17.8 us
  transfers between devices with their start and end apart: 6, of which 4 were waited for; matrix products, arithmetic and copies ran while one was open for 2% of the time, Pallas kernels for 0%

commit v1 on v0

--- a/solution.py
+++ b/solution.py
@@ -75,7 +75,9 @@
         lax.all_gather(place_column, "rows", axis=2, tiled=True),
     )
     state_full, place_full = (
-        lax.all_gather(state_own[0], "obs", axis=0, tiled=True),
+        jnp.concatenate(
+            lax.all_to_all(jnp.stack([state_own[0]] * lax.axis_size("obs")), "obs", 0, 0), axis=0
+        ),
         lax.all_gather(state_pos, "obs", axis=0, tiled=True),
     )
     first_block = lax.axis_index("rows") * ROW_BLOCKS

time: 593 us -> 563 us (0.949)
  waiting for transfers between devices: 279 us -> 232 us
  starting transfers between devices: 9.42 us -> 19 us
  blocking collectives: 71 us -> 77.4 us
    all_gather x1 -> x0, waiting for transfers between devices: 58.7 us -> none  [local(): lax.all_gather(state_own[0], 'obs', axis=0, tiled=True)]
    reduce_scatter x1, waiting for transfers between devices: 216 us -> 230 us  [local(): shares = lax.psum_scatter(summed, 'obs', scatter_dimension=0, tiled=True)]
    all_to_all x0 -> x1, starting transfers between devices: none -> 9.59 us  [local(): lax.all_to_all(jnp.stack([state_own[0]] * lax.axis_size('obs')), 'obs', 0...]
    unnamed x1, blocking collectives: 62.3 us -> 68.3 us
  transfers between devices with their start and end apart: 6 -> 6, of which waited for: 4 -> 2; matrix products, arithmetic and copies ran while one was open for 2% -> 2% of each run, Pallas kernels for 0% -> 0%
where the time goes in v1:
time: 563 us; the launch traced here: 559 us
  waiting for transfers between devices  232 us (41%)
  local copies, waits for them, and re-layouts  91.5 us (16%)
  blocking collectives  77.4 us (14%)
  matrix products  74.5 us (13%)
  other arithmetic  48.8 us (9%)
  starting transfers between devices  19 us (3%)
  between operations  14 us (2%)
    reduce_scatter x1, waiting for transfers between devices, local(): shares = lax.psum_scatter(summed, 'obs', scatter_dimension=0, tiled=True)  230 us
    unnamed x1, blocking collectives  68.3 us
    gather x32, local copies, waits for them, and re-layouts, visit(): gathered = state_tiles[blocks_here].reshape(-1, member_count)  57.8 us
    scatter-add x32, other arithmetic, visit(): running.at[blocks_here].add(additions.reshape(-1, edge_size, member_count))  42.6 us
    dot_general x32, matrix products, visit(): lax.dot_general(gathered, obs_tile, (((1,), (1,)), ((), ())), preferred_e...  38.7 us
    dot_general x32, matrix products, visit(): additions = jnp.dot(scaled, weight_tile, preferred_element_type=jnp.float32)  35.8 us
    gather x32, local copies, waits for them, and re-layouts, visit(): positions = place_tiles[blocks_here].reshape(-1)  17.8 us
  transfers between devices with their start and end apart: 6, of which 2 were waited for; matrix products, arithmetic and copies ran while one was open for 2% of the time, Pallas kernels for 0%

profile of v1, /device:TPU:1, one launch (start us, length us, event | category | flops | bytes accessed | tf_op | source)
XLA Modules:
  0.0 558.9 jit_solution(7591297065108748451)
XLA Ops:
  7.3 3.3 collective-permute-start
  10.6 2.0 stack.3
  12.5 9.6 %all-to-all-start = ((bf16[32,64,256]{2,1,0:T(8,128)(2,1)}), bf16[32,64,256]{2,1,0:T(8,128)(2,1)}, u32[]{:S(2)}, u32[]{:S(2)}) async-start(bf16[32,64,256]{2,1,0:T(8,128)(2,1)} %stack.3), calls=%async_computation | async-start | bytes 2097152 | tf_op jit(solution)/shard_map/all_to_all | solution.py:79
  26.8 68.3 %all-reduce = bf16[2048]{0:T(1024)(128)(2,1)S(1)} all-reduce(bf16[2048]{0:T(1024)(128)(2,1)S(1)} %dynamic-update-slice), channel_id=1, replica_groups=mesh['rows'=4,'half'=2,'obs'=32] {'obs'}, use_global_device_ids=true, to_apply=%add | all-reduce | flops 2048 | bytes 8192
  95.1 9.2 %all-gather = bf16[2,2048]{1,0:T(2,128)(2,1)S(1)} all-gather(bf16[2,512]{1,0:T(2,128)(2,1)S(1)} %copy-done.3), channel_id=2, replica_groups=mesh['rows'=4,'half'=2,'obs'=32] {'rows'}, dimensions={1}, use_global_device_ids=true | all-gather | bytes 10240 | tf_op jit(solution)/shard_map/all_gather | solution.py:75
  105.5 3.0 fusion.36
  108.6 3.0 fusion.35
  111.8 99.0 %while.21 = (s32[]{:T(128)}, f32[16,128,256]{2,1,0:T(8,128)S(1)}, s32[16,8]{1,0:T(8,128)S(1)}, bf16[16,128,256]{2,1,0:T(8,128)(2,1)}, bf16[16,128,256]{2,1,0:T(8...) while((s32[]{:T(128)}, f32[16,128,256]{2,1,0:T(8,128)S(1)}, ...), condition=%wide.region_13.14_spmd, body=%wide.region_11.13_spmd.sunk | while | flops 135267360 | bytes 6450065 | solution.py:64
  111.8 1.8 gather_fusion.2
  118.0 1.8 gather_fusion.2
  124.2 1.8 gather_fusion.2
  130.4 1.8 gather_fusion.2
  136.6 1.8 gather_fusion.2
  142.8 1.8 gather_fusion.2
  155.2 1.8 gather_fusion.2
  167.6 1.8 gather_fusion.2
  173.7 1.8 gather_fusion.2
  179.9 1.8 gather_fusion.2
  186.1 1.8 gather_fusion.2
  198.5 1.8 gather_fusion.2
  212.4 99.1 %while.20 = (s32[]{:T(128)}, f32[16,128,256]{2,1,0:T(8,128)S(1)}, s32[16,8]{1,0:T(8,128)S(1)}, bf16[16,128,256]{2,1,0:T(8,128)(2,1)}, bf16[16,128,256]{2,1,0:T(8...) while((s32[]{:T(128)}, f32[16,128,256]{2,1,0:T(8,128)S(1)}, ...), condition=%wide.region_6.7_spmd, body=%wide.region_4.6_spmd.sunk | while | flops 135267360 | bytes 6450065 | solution.py:64
  311.5 3.3 add.105
  314.8 229.8 %reduce-scatter.2.cloned.1.call-done = f32[64,256]{1,0:T(8,128)} async-done(((f32[2048,256]{1,0:T(8,128)}), f32[64,256]{1,0:T(8,128)}) %reduce-scatter.2.cloned.1.call-update) | async-done | bytes 65552 | tf_op jit(solution)/shard_map/reduce_scatter | solution.py:106
  544.6 6.0 %collective-permute-start.1 = (f32[64,256]{1,0:T(8,128)}, f32[64,256]{1,0:T(8,128)S(1)}, u32[]{:S(2)}, u32[]{:S(2)}) collective-permute-start(f32[64,256]{1,0:T(8,128)} %reduce-scatter.2.cloned.1.call-done), channel_id=1, source_target_pairs={{0,32},{32,0},{1,33},{33,1},{2,34},{34,2},{3,35},{35,3},{4,36},{36... | collective-permute-start | bytes 196616 | tf_op jit(solution)/shard_map/ppermute | solution.py:14
  (358 shorter events, 183.8 us)
Async XLA Ops:
  6.5 16.7 %copy-start.2 = (s32[2,512,16]{1,2,0:T(8,128)S(1)}, s32[2,512,16]{1,2,0:T(8,128)}, u32[]{:S(2)}) copy-start(s32[2,512,16]{1,2,0:T(8,128)} %param.15) | copy-start | bytes 196612
  6.5 99.0 %all-gather.4.cloned.1.call-start = ((), (), s32[]{:S(2)}) async-start(), calls=%async_computation.2 | async-start | bytes 2621440 | tf_op jit(solution)/shard_map/all_gather | solution.py:73
  7.3 14.9 %collective-permute-start = (bf16[2,1,512,256]{3,2,1,0:T(8,128)(2,1)}, bf16[2,1,512,256]{3,2,1,0:T(8,128)(2,1)S(1)}, u32[]{:S(2)}, u32[]{:S(2)}) collective-permute-start(bf16[2,1,512,256]{3,2,1,0:T(8,128)(2,1)} %param.14), channel_id=1, source_target_pairs={{0,32},{32,0},{1,33},{33,1},{2,34},{34,2},{3,35},{35,3},{4,36},{36... | collective-permute-start | bytes 1572872 | tf_op jit(solution)/shard_map/ppermute | solution.py:14
  10.5 14.7 %copy-start.5 = (u32[256]{0:T(256)S(1)}, u32[256]{0:T(256)}, u32[]{:S(2)}) copy-start(u32[256]{0:T(256)} %constant.78) | copy-start | bytes 3076
  10.5 16.0 %copy-start.4 = (bf16[64]{0:T(256)(128)(2,1)S(1)}, bf16[64]{0:T(256)(128)(2,1)}, u32[]{:S(2)}) copy-start(bf16[64]{0:T(256)(128)(2,1)} %param.11) | copy-start | bytes 388
  12.5 82.5 %copy-start.3 = (bf16[2,512]{1,0:T(2,128)(2,1)S(1)}, bf16[2,512]{1,0:T(2,128)(2,1)}, u32[]{:S(2)}) copy-start(bf16[2,512]{1,0:T(2,128)(2,1)} %param.13) | copy-start | bytes 6148
  12.5 99.1 %all-to-all-start = ((bf16[32,64,256]{2,1,0:T(8,128)(2,1)}), bf16[32,64,256]{2,1,0:T(8,128)(2,1)}, u32[]{:S(2)}, u32[]{:S(2)}) async-start(bf16[32,64,256]{2,1,0:T(8,128)(2,1)} %stack.3), calls=%async_computation | async-start | bytes 2097152 | tf_op jit(solution)/shard_map/all_to_all | solution.py:79
  22.1 86.4 %all-gather.6.cloned.1.call-start = ((), (), s32[]{:S(2)}) async-start(), calls=%async_computation.3 | async-start | bytes 2621440 | tf_op jit(solution)/shard_map/all_gather | solution.py:74
  22.2 0.8 copy-start.1
  23.0 521.6 %reduce-scatter.2.cloned.1.call-start = ((), (), s32[]{:S(2)}) async-start(), calls=%async_computation.4 | async-start | bytes 2162688 | tf_op jit(solution)/shard_map/reduce_scatter | solution.py:106
  210.8 1.4 copy-start
  544.6 7.1 %collective-permute-start.1 = (f32[64,256]{1,0:T(8,128)}, f32[64,256]{1,0:T(8,128)S(1)}, u32[]{:S(2)}, u32[]{:S(2)}) collective-permute-start(f32[64,256]{1,0:T(8,128)} %reduce-scatter.2.cloned.1.call-done), channel_id=1, source_target_pairs={{0,32},{32,0},{1,33},{33,1},{2,34},{34,2},{3,35},{35,3},{4,36},{36... | collective-permute-start | bytes 196616 | tf_op jit(solution)/shard_map/ppermute | solution.py:14
Sparse Core Ops, SparseCore 0:
  9.1 37.0 all-gather.3
  48.0 33.3 all-gather.5
  314.9 229.6 reduce-scatter.1
